TPU v7x, 32 devices: a whole 2x2x4 slice. The times are simulated.
32 devices in a mesh: member: 8 (over z, y), grid: 4 (over x, core).
Axes of the slice: x: 2, y: 2, z: 4, core: 2. Of those that a mesh axis runs over, the one named last changes fastest.
Arguments:
- latents: bfloat16 [16, 4096, 1024], P('member', 'grid'), may hold values from -6 to 6
- w_in: bfloat16 [1024, 1024], replicated, may hold values from -0.1875 to 0.1875
- b_in: float32 [1024], replicated, may hold values from -3 to 3
- w_out: bfloat16 [1024, 96], replicated, may hold values from -0.1875 to 0.1875
- b_out: float32 [96], replicated, may hold values from -3 to 3
- target: float32 [96, 4096], P('member', 'grid'), may hold values from -6 to 6
- area_weight: float32 [4096], P('grid'), may hold values from 0.25 to 10
- var_weight: float32 [96], P('member'), may hold values from 0.25 to 10
- smoothers: float32 [2, 32, 4, 128, 128], P(None, 'grid'), may hold values from -0.25 to 0.25
- block_index: int32 [2, 32, 4], P(None, 'grid'), may hold values from 0 to 31, as said below
- block_count: int32 [2, 32], P(None, 'grid'), may hold values from 1 to 4, as said below
Outputs:
- grad_latent: bfloat16 [16, 4096, 1024], P('member', 'grid')
- loss: float32 [], replicated
Inputs may be any that keep to these rules, and one draw needn't show every extreme that they name: `block_index`: block row r lists blocks that lie at most 8 blocks from r on either side; that distance is reached on both sides in some rows; entries of a row may repeat. Only the first block_count[s, r] slots of block row r are used.
All inputs are finite; a program needn't handle non-finite values.
Results may differ from a plain program's by a relative error of at most 0.008.
Values may be sent and summed in bfloat16 or wider, within the bound.
No kernel may reach another device: no remote copies, remote signals or barrier semaphores. Data moves between devices by JAX's collectives and lax.ppermute only.
A program may use at most 64 MiB of HBM per device.

v0:
```python
import functools
import math

import jax
import jax.numpy as jnp
import numpy as np
from jax import lax
from jax.experimental import pallas as pl
from jax.experimental.pallas import tpu as pltpu
from jax.sharding import PartitionSpec as P

kernel_eps = 0.01
f32 = jnp.float32
bf16 = jnp.bfloat16
SUB = 8
GELU_C = math.sqrt(2.0 / math.pi)
GELU_A = 0.044715
VMEM_LIMIT = 60 * 1024 * 1024


class Layout:
    def __init__(self, senders, own_members, variables, blocks, block):
        self.senders = senders
        self.own = own_members
        self.vars = variables
        self.blocks = blocks
        self.block = block
        rest = variables % SUB
        self.half = 0 < rest <= SUB // 2 and own_members % 2 == 0 and blocks % 2 == 0
        self.whole = variables // SUB if self.half or rest == 0 else variables // SUB + 1
        self.piece = own_members * (self.whole * SUB + (SUB // 2 if self.half else 0))
        self.rows = senders * self.piece
        self.members = senders * own_members
        self.tiles = blocks * self.whole + (blocks // 2 if self.half else 0)
        self.truth_rows = -(-variables // 16) * 16
        self.total_rows = self.rows + self.truth_rows

    def permutation(self):
        out = np.zeros((self.own, self.senders * self.vars, self.rows), np.float32)
        for sender in range(self.senders):
            for c in range(self.piece):
                if c < self.whole * self.own * SUB:
                    v = c // (self.own * SUB) * SUB + c % SUB
                    m = c // SUB % self.own
                else:
                    tail = c - self.whole * self.own * SUB
                    v = self.whole * SUB + tail % (SUB // 2)
                    m = tail // (SUB // 2)
                if v < self.vars:
                    out[m, sender * self.vars + v, sender * self.piece + c] = 1.0
        return out


def low_half():
    return lax.broadcasted_iota(jnp.int32, (SUB, 128), 0) < SUB // 2


def swap(x):
    return pltpu.roll(x, SUB // 2, 0)


def rows_to_tiles(lay, take, put, put_truth):
    step = 2 if lay.half else 1
    for r0 in range(0, lay.blocks, step):
        rows = [take(r0 + d) for d in range(step)]
        for d in range(step):
            for a in range(lay.whole):
                t = (r0 + d) * lay.whole + a
                for sender in range(lay.senders):
                    for m in range(lay.own):
                        at = sender * lay.piece + (a * lay.own + m) * SUB
                        put(t, sender * lay.own + m, rows[d][at : at + SUB])
                at = lay.rows + a * SUB
                put_truth(t, rows[d][at : at + SUB])
        if lay.half:
            t = lay.blocks * lay.whole + r0 // 2
            low = low_half()
            for sender in range(lay.senders):
                for m in range(0, lay.own, 2):
                    at = sender * lay.piece + lay.whole * lay.own * SUB + m * (SUB // 2)
                    first, second = rows[0][at : at + SUB], rows[1][at : at + SUB]
                    put(t, sender * lay.own + m, jnp.where(low, first, swap(second)))
                    put(t, sender * lay.own + m + 1, jnp.where(low, swap(first), second))
            at = lay.rows + lay.whole * SUB
            first, second = rows[0][at : at + SUB], rows[1][at : at + SUB]
            put_truth(t, jnp.where(low, first, swap(second)))


def tiles_to_rows(lay, get, put):
    for r in range(lay.blocks):
        for sender in range(lay.senders):
            for a in range(lay.whole):
                for m in range(lay.own):
                    at = sender * lay.piece + (a * lay.own + m) * SUB
                    put(r, at, get(r * lay.whole + a, sender * lay.own + m))
            if lay.half:
                t = lay.blocks * lay.whole + r // 2
                low = low_half()
                for m in range(0, lay.own, 2):
                    at = sender * lay.piece + lay.whole * lay.own * SUB + m * (SUB // 2)
                    first = get(t, sender * lay.own + m)
                    second = get(t, sender * lay.own + m + 1)
                    if r % 2 == 0:
                        put(r, at, jnp.where(low, first, swap(second)))
                    else:
                        put(r, at, jnp.where(low, swap(first), second))


def crps_tile(x, y, w):
    members = len(x)
    pair_total = None
    pulls = [None] * members
    for i in range(members):
        for j in range(i + 1, members):
            d = x[i] - x[j]
            t = d * d + kernel_eps
            inv = lax.rsqrt(t)
            k = t * inv
            dk = d * inv
            pair_total = k if pair_total is None else pair_total + k
            pulls[i] = dk if pulls[i] is None else pulls[i] + dk
            pulls[j] = -dk if pulls[j] is None else pulls[j] - dk
    miss_total = None
    grads = []
    for i in range(members):
        d = x[i] - y
        t = d * d + kernel_eps
        inv = lax.rsqrt(t)
        k = t * inv
        miss_total = k if miss_total is None else miss_total + k
        grads.append(w * (d * inv - pulls[i] * (1.0 / (members - 1))))
    score = miss_total * (1.0 / members) - pair_total * (1.0 / (members * (members - 1)))
    return w * score, grads


def crps_loop(lay, x_ref, y_ref, w_ref, total_ref):
    def step(t, total):
        x = [x_ref[t, m] for m in range(lay.members)]
        part, grads = crps_tile(x, y_ref[t], w_ref[t])
        for m in range(lay.members):
            x_ref[t, m] = grads[m]
        return total + part

    total_ref[...] = lax.fori_loop(0, lay.tiles, step, total_ref[...])


def fwd_kernel(lay, lat_ref, w_in_ref, b_in_ref, w_out_ref, perm_ref, b_out_ref, hi_ref, lo_ref, pre_ref, a_scr, bias_scr):
    @pl.when(pl.program_id(0) == 0)
    def _():
        spread = None
        for m in range(lay.own):
            p = perm_ref[m]
            a_scr[m] = jnp.dot(w_out_ref[...], p, preferred_element_type=f32).astype(bf16)
            spread = p.astype(f32) if spread is None else spread + p.astype(f32)
        bias = jnp.broadcast_to(b_out_ref[...], (SUB, b_out_ref.shape[1]))
        bias_scr[...] = jnp.dot(bias, spread, precision=lax.Precision.HIGHEST, preferred_element_type=f32)

    acc = bias_scr[0:1, :]
    for m in range(lay.own):
        pre = jnp.dot(lat_ref[m], w_in_ref[...], preferred_element_type=f32) + b_in_ref[...]
        pre_ref[m] = pre.astype(bf16)
        inner = pre * (GELU_C + (GELU_C * GELU_A) * (pre * pre))
        half = 0.5 * pre
        hidden = (half + half * jnp.tanh(inner)).astype(bf16)
        acc = acc + jnp.dot(hidden, a_scr[m], preferred_element_type=f32)
    field = acc.T
    for sender in range(lay.senders):
        for r in range(hi_ref.shape[1]):
            part = field[sender * lay.piece : (sender + 1) * lay.piece, r * lay.block : (r + 1) * lay.block]
            hi = part.astype(bf16)
            hi_ref[sender, r] = hi
            lo_ref[sender, r] = (part - hi.astype(f32)).astype(bf16)


def prep_kernel(lay, slots, count_ref, pre_ref, w_in_ref, w_out_ref, permt_ref, sm_ref, slope_ref, w_int_ref, at_ref, wb_ref):
    x = pre_ref[...].astype(f32)
    sq = x * x
    t = jnp.tanh(x * (GELU_C + (GELU_C * GELU_A) * sq))
    half = 0.5 * (1.0 + t)
    tail = (0.5 * x) * (1.0 - t * t) * (GELU_C + (3.0 * GELU_C * GELU_A) * sq)
    slope_ref[...] = (half + tail).astype(bf16)
    w_int_ref[...] = w_in_ref[...].T
    scales, rows = sm_ref.shape[0], sm_ref.shape[1]
    step = pl.program_id(0)
    for s in range(scales):
        for r in range(rows):
            for k in range(slots):
                live = (k < count_ref[s, step * rows + r]).astype(f32)
                wb_ref[s, r, k * lay.block : (k + 1) * lay.block, :] = (sm_ref[s, r, k] * live).astype(bf16)

    for m in range(lay.own):
        at_ref[m] = lax.dot_general(
            permt_ref[m], w_out_ref[...], (((1,), (1,)), ((), ())), preferred_element_type=f32
        ).astype(bf16)


def raw_kernel(lay, vw_ref, area_ref, hi_ref, lo_ref, target_ref, grad_ref, w_ref, total_ref, x_scr, y_scr):
    rows = lax.broadcasted_iota(jnp.int32, (lay.truth_rows, lay.block), 0)
    column = jnp.zeros((lay.truth_rows, lay.block), f32)
    for v in range(lay.vars):
        column = jnp.where(rows == v, vw_ref[v], column)

    def weights(r):
        return column * area_ref[:, r * lay.block : (r + 1) * lay.block]

    def take(r):
        field = hi_ref[:, r].astype(f32) + lo_ref[:, r].astype(f32)
        truth = target_ref[:, r * lay.block : (r + 1) * lay.block]
        return jnp.concatenate([field.reshape(lay.rows, lay.block), truth], 0)

    def put(t, m, tile):
        x_scr[t, m] = tile

    def put_truth(t, tile):
        y_scr[t] = tile

    def put_weight(t, tile):
        w_ref[t] = tile

    rows_to_tiles(lay, take, put, put_truth)
    for r in range(lay.blocks):
        w = weights(r)
        for a in range(lay.whole):
            w_ref[r * lay.whole + a] = w[a * SUB : (a + 1) * SUB]
        if lay.half and r % 2:
            low = low_half()
            at = lay.whole * SUB
            first, second = weights(r - 1)[at : at + SUB], w[at : at + SUB]
            w_ref[lay.blocks * lay.whole + r // 2] = jnp.where(low, first, swap(second))
    total_ref[...] = jnp.zeros_like(total_ref)
    crps_loop(lay, x_scr, y_scr, w_ref, total_ref)

    def put_rows(r, at, tile):
        grad_ref[r, at : at + SUB] = tile

    tiles_to_rows(lay, lambda t, m: x_scr[t, m], put_rows)


def scales_kernel(lay, slots, pos_ref, left_ref, own_ref, right_ref, tl_ref, to_ref, tr_ref, wb_ref, w_ref, base_ref, total_in_ref, center_ref, lower_ref, upper_ref, loss_ref, ext_scr, x_scr, y_scr, total_scr, row_scr, adj_scr):
    scales = wb_ref.shape[0]
    block = lay.block
    for at, (src, truth) in enumerate(((left_ref, tl_ref), (own_ref, to_ref), (right_ref, tr_ref))):
        for r in range(lay.blocks):
            field = src[:, r].astype(f32).reshape(lay.rows, block)
            ext_scr[at * lay.blocks + r, : lay.rows] = field.astype(bf16)
            ext_scr[at * lay.blocks + r, lay.rows :] = truth[:, r * block : (r + 1) * block]
    adj_scr[...] = jnp.zeros_like(adj_scr)
    total_scr[...] = total_in_ref[...]
    for s in range(scales):

        def take(r):
            gathered = jnp.concatenate([ext_scr[pos_ref[s, r, k]] for k in range(slots)], 1)
            return jnp.dot(gathered, wb_ref[s, r], preferred_element_type=f32)

        def put(t, m, tile):
            x_scr[t, m] = tile

        def put_truth(t, tile):
            y_scr[t] = tile

        rows_to_tiles(lay, take, put, put_truth)
        crps_loop(lay, x_scr, y_scr, w_ref, total_scr)

        def put_rows(r, at, tile):
            row_scr[r, at : at + SUB] = tile

        tiles_to_rows(lay, lambda t, m: x_scr[t, m], put_rows)
        for r in range(lay.blocks):
            back = lax.dot_general(
                row_scr[r].astype(bf16), wb_ref[s, r], (((1,), (1,)), ((), ())), preferred_element_type=f32
            )
            for k in range(slots):
                p = pos_ref[s, r, k]
                adj_scr[p] = adj_scr[p] + back[:, k * block : (k + 1) * block]
    n = lay.blocks
    lower_ref[...] = adj_scr[0:n].astype(bf16)
    center_ref[...] = adj_scr[n : 2 * n] + base_ref[...]
    upper_ref[...] = adj_scr[2 * n : 3 * n].astype(bf16)
    loss_ref[...] = jnp.broadcast_to(jnp.sum(total_scr[...]), loss_ref.shape)


def join_kernel(lay, center_ref, a_ref, b_ref, out_ref):
    for r in range(lay.blocks):
        rows = center_ref[r] + (a_ref[r].astype(f32) + b_ref[r].astype(f32))
        out_ref[:, r] = rows.reshape(lay.senders, lay.piece, lay.block).astype(bf16)


def bwd_kernel(lay, g_ref, at_ref, slope_ref, w_int_ref, out_ref):
    cols = []
    for r in range(g_ref.shape[1]):
        rows = g_ref[:, r].astype(f32).reshape(lay.rows, lay.block)
        cols.append(rows.T.astype(bf16))
    grads = jnp.concatenate(cols, 0)
    for m in range(lay.own):
        hidden_grad = jnp.dot(grads, at_ref[m], preferred_element_type=f32)
        pre_grad = (hidden_grad * slope_ref[m].astype(f32)).astype(bf16)
        out_ref[m] = jnp.dot(pre_grad, w_int_ref[...], preferred_element_type=f32).astype(bf16)


def params():
    return pltpu.CompilerParams(vmem_limit_bytes=VMEM_LIMIT)


def cost(flops, nbytes, trans=0):
    return pl.CostEstimate(flops=int(flops), bytes_accessed=int(nbytes), transcendentals=int(trans))


VM = pl.BlockSpec(memory_space=pltpu.VMEM)
SM = pl.BlockSpec(memory_space=pltpu.SMEM)


def whole_spec(shape):
    return pl.BlockSpec(shape, lambda i: (0,) * len(shape))


def on_device(
    latents,
    w_in,
    b_in,
    w_out,
    b_out,
    target,
    area_weight,
    var_weight,
    smoothers,
    block_index,
    block_count,
):
    own, points, width = latents.shape
    hidden_width = w_in.shape[1]
    var_total = w_out.shape[1]
    var_local = target.shape[0]
    scales, blocks, slots, block, _ = smoothers.shape
    senders = lax.axis_size("member")
    devices_grid = lax.axis_size("grid")
    lay = Layout(senders, own, var_local, blocks, block)
    perm_np = lay.permutation()
    perm = jnp.asarray(perm_np, bf16)
    perm_t = jnp.asarray(perm_np.transpose(0, 2, 1), bf16)
    payload = (senders, blocks, lay.piece, block)

    tile = min(points, 256)
    steps = points // tile
    tile_blocks = tile // block
    payload_spec = pl.BlockSpec((senders, tile_blocks, lay.piece, block), lambda i: (0, i, 0, 0))
    wide_spec = pl.BlockSpec((own, tile, hidden_width), lambda i: (0, i, 0))
    hi, lo, pre = pl.pallas_call(
        functools.partial(fwd_kernel, lay),
        grid=(steps,),
        in_specs=[
            pl.BlockSpec((own, tile, width), lambda i: (0, i, 0)),
            whole_spec(w_in.shape),
            whole_spec((1, hidden_width)),
            whole_spec(w_out.shape),
            whole_spec(perm.shape),
            whole_spec((1, var_total)),
        ],
        out_specs=[payload_spec, payload_spec, wide_spec],
        out_shape=[
            jax.ShapeDtypeStruct(payload, bf16),
            jax.ShapeDtypeStruct(payload, bf16),
            jax.ShapeDtypeStruct((own, points, hidden_width), bf16),
        ],
        scratch_shapes=[pltpu.VMEM((own, hidden_width, lay.rows), bf16), pltpu.VMEM((SUB, lay.rows), f32)],
        compiler_params=params(),
        cost_estimate=cost(2 * own * points * width * hidden_width, 12e6, own * points * hidden_width),
        name="fwd",
    )(latents, w_in, b_in.reshape(1, -1), w_out, perm, b_out.reshape(1, -1))

    own_hi = lax.all_to_all(hi, "member", split_axis=0, concat_axis=0, tiled=True)
    own_lo = lax.all_to_all(lo, "member", split_axis=0, concat_axis=0, tiled=True)

    prep_steps = math.gcd(blocks, 4)
    prep_rows = blocks // prep_steps
    prep_tile = points // prep_steps
    prep_cols = hidden_width // prep_steps
    slope, w_in_t, a_t, wb = pl.pallas_call(
        functools.partial(prep_kernel, lay, slots),
        grid=(prep_steps,),
        in_specs=[
            SM,
            pl.BlockSpec((own, prep_tile, hidden_width), lambda i: (0, i, 0)),
            pl.BlockSpec((width, prep_cols), lambda i: (0, i)),
            pl.BlockSpec((prep_cols, var_total), lambda i: (i, 0)),
            whole_spec(perm_t.shape),
            pl.BlockSpec((scales, prep_rows, slots, block, block), lambda i: (0, i, 0, 0, 0)),
        ],
        out_specs=[
            pl.BlockSpec((own, prep_tile, hidden_width), lambda i: (0, i, 0)),
            pl.BlockSpec((prep_cols, width), lambda i: (i, 0)),
            pl.BlockSpec((own, lay.rows, prep_cols), lambda i: (0, 0, i)),
            pl.BlockSpec((scales, prep_rows, slots * block, block), lambda i: (0, i, 0, 0)),
        ],
        out_shape=[
            jax.ShapeDtypeStruct((own, points, hidden_width), bf16),
            jax.ShapeDtypeStruct((hidden_width, width), bf16),
            jax.ShapeDtypeStruct((own, lay.rows, hidden_width), bf16),
            jax.ShapeDtypeStruct((scales, blocks, slots * block, block), bf16),
        ],
        compiler_params=params(),
        cost_estimate=cost(2e9, 2e7, own * points * hidden_width),
        name="prep",
    )(block_count, pre, w_in, w_out, perm_t, smoothers)

    _, target = lax.optimization_barrier((pre, target))
    target_pad = jnp.pad(target, ((0, lay.truth_rows - var_local), (0, 0)))
    truth = target_pad.astype(bf16)
    up = [(i, i + 1) for i in range(devices_grid - 1)]
    down = [(i + 1, i) for i in range(devices_grid - 1)]
    truth_left = lax.ppermute(truth, "grid", up)
    truth_right = lax.ppermute(truth, "grid", down)
    field_left = lax.ppermute(own_hi, "grid", up)
    field_right = lax.ppermute(own_hi, "grid", down)

    grad_shape = (blocks, lay.rows, block)
    tile_shape = (lay.tiles, lay.members, SUB, block)
    base, w_tiles, total = pl.pallas_call(
        functools.partial(raw_kernel, lay),
        in_specs=[SM, VM, VM, VM, VM],
        out_specs=[VM, VM, VM],
        out_shape=[
            jax.ShapeDtypeStruct(grad_shape, f32),
            jax.ShapeDtypeStruct((lay.tiles, SUB, block), f32),
            jax.ShapeDtypeStruct((SUB, block), f32),
        ],
        scratch_shapes=[pltpu.VMEM(tile_shape, f32), pltpu.VMEM((lay.tiles, SUB, block), f32)],
        compiler_params=params(),
        cost_estimate=cost(5e8, 3e6, 2e6),
        name="raw",
    )(var_weight, area_weight.reshape(1, -1), own_hi, own_lo, target_pad)

    positions = jnp.clip(block_index - (lax.axis_index("grid") - 1) * blocks, 0, 3 * blocks - 1)
    device_count = senders * devices_grid
    center, lower, upper, losses = pl.pallas_call(
        functools.partial(scales_kernel, lay, slots),
        in_specs=[SM] + [VM] * 10,
        out_specs=[VM] * 4,
        out_shape=[
            jax.ShapeDtypeStruct(grad_shape, f32),
            jax.ShapeDtypeStruct(grad_shape, bf16),
            jax.ShapeDtypeStruct(grad_shape, bf16),
            jax.ShapeDtypeStruct((device_count, block), f32),
        ],
        scratch_shapes=[
            pltpu.VMEM((3 * blocks, lay.total_rows, block), bf16),
            pltpu.VMEM(tile_shape, f32),
            pltpu.VMEM((lay.tiles, SUB, block), f32),
            pltpu.VMEM((SUB, block), f32),
            pltpu.VMEM(grad_shape, f32),
            pltpu.VMEM((3 * blocks, lay.rows, block), f32),
        ],
        compiler_params=params(),
        cost_estimate=cost(2e9, 8e6, 4e6),
        name="scales",
    )(positions, field_left, own_hi, field_right, truth_left, truth, truth_right, wb, w_tiles, base, total)

    from_upper = lax.ppermute(lower, "grid", down)
    from_lower = lax.ppermute(upper, "grid", up)
    joined = pl.pallas_call(
        functools.partial(join_kernel, lay),
        in_specs=[VM] * 3,
        out_specs=VM,
        out_shape=jax.ShapeDtypeStruct(payload, bf16),
        compiler_params=params(),
        cost_estimate=cost(1e6, 2e6),
        name="join",
    )(center, from_upper, from_lower)
    field_grad = lax.all_to_all(joined, "member", split_axis=0, concat_axis=0, tiled=True)
    parts = lax.all_to_all(losses, ("member", "grid"), split_axis=0, concat_axis=0, tiled=True)
    loss = jnp.sum(parts[:, 0]) / ((scales + 1) * var_total * points * devices_grid)

    grad = pl.pallas_call(
        functools.partial(bwd_kernel, lay),
        grid=(steps,),
        in_specs=[
            payload_spec,
            whole_spec(a_t.shape),
            wide_spec,
            whole_spec(w_in_t.shape),
        ],
        out_specs=pl.BlockSpec((own, tile, width), lambda i: (0, i, 0)),
        out_shape=jax.ShapeDtypeStruct((own, points, width), bf16),
        compiler_params=params(),
        cost_estimate=cost(2 * own * points * width * hidden_width, 12e6),
        name="bwd",
    )(field_grad, a_t, slope, w_in_t)
    return grad, loss


def solution(mesh):
    in_specs = (
        P("member", "grid", None),
        P(),
        P(),
        P(),
        P(),
        P("member", "grid"),
        P("grid"),
        P("member"),
        P(None, "grid", None, None, None),
        P(None, "grid", None),
        P(None, "grid"),
    )
    out_specs = (P("member", "grid", None), P())
    return jax.shard_map(
        on_device, mesh=mesh, in_specs=in_specs, out_specs=out_specs, check_vma=False
    )
```

profile of v0, /device:TPU:0, one launch (start us, length us, event | category | flops | bytes accessed | tf_op | source)
XLA Modules:
  0.0 123.8 jit_solution(10843903275319379056)
XLA Ops:
  0.6 1.8 %copy.19.w_out_ref = bf16[1024,96]{1,0:T(8,128)(2,1)} copy(bf16[1024,96]{0,1:T(8,128)(2,1)} %param.16) | data formatting | bytes 393216 | tf_op args[3]
  2.4 11.8 %fwd.1 = (bf16[8,8,24,128]{3,2,1,0:T(8,128)(2,1)}, bf16[8,8,24,128]{3,2,1,0:T(8,128)(2,1)}, bf16[2,1024,1024]{2,1,0:T(8,128)(2,1)}) custom-call(bf16[2,1024,1024]{2,1,0:T(8,128)(2,1)} %lat_ref.1, bf16[1024,1024]{1,0:T(8,128)(2,1)} %w_in_ref.3, f32[1,1024]{1,0:T(1,128)} %bitcast.9, bf16[1024,96]{1,0:T(8,128)(2,1)} %copy.19.w_out_ref, ...), custom_call_target="tpu_custom_call" | custom-call | flops 4294967296 | bytes 12000000 | tf_op jit(solution)/shard_map/fwd/pallas_call | solution.py:347
  14.2 19.4 %all_to_all.27.hi_ref.own_ref = bf16[8,8,24,128]{3,2,1,0:T(8,128)(2,1)S(1)} all-to-all(bf16[8,8,24,128]{3,2,1,0:T(8,128)(2,1)} %get-tuple-element.17), channel_id=1, replica_groups=mesh['member'=8,'grid'=4] {'member'}, dimensions={0} | all-to-all | bytes 786432 | tf_op jit(solution)/shard_map/all_to_all | solution.py:370
  33.6 3.5 %all-to-all-start.1 = ((bf16[8,8,24,128]{3,2,1,0:T(8,128)(2,1)}), bf16[8,8,24,128]{3,2,1,0:T(8,128)(2,1)S(1)}, u32[]{:S(2)}, u32[]{:S(2)}) async-start(bf16[8,8,24,128]{3,2,1,0:T(8,128)(2,1)} %get-tuple-element.21), calls=%async_computation.1 | async-start | bytes 786432 | tf_op jit(solution)/shard_map/all_to_all | solution.py:371
  37.1 1.3 %collective-permute-start.2 = (bf16[16,1024]{1,0:T(8,128)(2,1)S(1)}, bf16[16,1024]{1,0:T(8,128)(2,1)S(1)}, u32[]{:S(2)}, u32[]{:S(2)}) collective-permute-start(bf16[16,1024]{1,0:T(8,128)(2,1)S(1)} %pad.6.to_ref), channel_id=1, source_target_pairs={{0,1},{1,2},{2,3},{4,5},{5,6},{6,7},{8,9},{9,10},{10,11},{12,13},{... | collective-permute-start | bytes 98312 | tf_op jit(solution)/shard_map/ppermute | solution.py:410
  38.4 1.3 %collective-permute-start.3 = (bf16[16,1024]{1,0:T(8,128)(2,1)S(1)}, bf16[16,1024]{1,0:T(8,128)(2,1)S(1)}, u32[]{:S(2)}, u32[]{:S(2)}) collective-permute-start(bf16[16,1024]{1,0:T(8,128)(2,1)S(1)} %pad.6.to_ref), channel_id=1, source_target_pairs={{1,0},{2,1},{3,2},{5,4},{6,5},{7,6},{9,8},{10,9},{11,10},{13,12},{... | collective-permute-start | bytes 98312 | tf_op jit(solution)/shard_map/ppermute | solution.py:411
  39.7 0.6 pad.4.target_ref
  40.3 0.1 copy.18
  40.4 4.8 %collective-permute-start = (bf16[8,8,24,128]{3,2,1,0:T(8,128)(2,1)S(1)}, bf16[8,8,24,128]{3,2,1,0:T(8,128)(2,1)S(1)}, u32[]{:S(2)}, u32[]{:S(2)}) collective-permute-start(bf16[8,8,24,128]{3,2,1,0:T(8,128)(2,1)S(1)} %all_to_all.27.hi_ref.own_ref), channel_id=1, source_target_pairs={{0,1},{1,2},{2,3},{4,5},{5,6},{6,7},{8,9},{9,10},{10,11},{12,13},{... | collective-permute-start | bytes 1179656 | tf_op jit(solution)/shard_map/ppermute | solution.py:412
  45.2 1.3 %collective-permute-start.1 = (bf16[8,8,24,128]{3,2,1,0:T(8,128)(2,1)S(1)}, bf16[8,8,24,128]{3,2,1,0:T(8,128)(2,1)S(1)}, u32[]{:S(2)}, u32[]{:S(2)}) collective-permute-start(bf16[8,8,24,128]{3,2,1,0:T(8,128)(2,1)S(1)} %all_to_all.27.hi_ref.own_ref), channel_id=1, source_target_pairs={{1,0},{2,1},{3,2},{5,4},{6,5},{7,6},{9,8},{10,9},{11,10},{13,12},{... | collective-permute-start | bytes 1179656 | tf_op jit(solution)/shard_map/ppermute | solution.py:413
  46.5 13.4 %prep.1 = (bf16[2,1024,1024]{2,1,0:T(8,128)(2,1)}, bf16[1024,1024]{1,0:T(8,128)(2,1)}, bf16[2,192,1024]{2,1,0:T(8,128)(2,1)}, bf16[2,8,512,128]{3,2,1,0:T(8,128)(2,1)}) custom-call(s32[2,8]{1,0:T(2,128)} %count_ref.1, bf16[2,1024,1024]{2,1,0:T(8,128)(2,1)} %get-tuple-element.18.pre_ref, bf16[1024,1024]{1,0:T(8,128)(2,1)} %w_in_ref.3, ...), custom_call_target="tpu_custom_call" | custom-call | flops 2000000000 | bytes 20000000 | tf_op jit(solution)/shard_map/prep/pallas_call | solution.py:377
  59.9 0.6 subtract_clamp_fusion.pos_ref
  60.5 0.7 copy-done.1
  61.3 4.3 %raw.1 = (f32[8,192,128]{2,1,0:T(8,128)}, f32[12,8,128]{2,1,0:T(8,128)}, f32[8,128]{1,0:T(8,128)}) custom-call(f32[12]{0:T(128)} %vw_ref.1, f32[1,1024]{1,0:T(1,128)} %bitcast.10, bf16[8,8,24,128]{3,2,1,0:T(8,128)(2,1)} %copy-done, bf16[8,8,24,128]{3,2,1,0:T(8,128)(2,1)} %copy-done.1, f32[16,1024]{1,0:T(8,128)} %pad.4.target_ref), custom_call_target="tpu_custom_call" | custom-call | flops 500000000 | bytes 3000000 | tf_op jit(solution)/shard_map/raw/pallas_call | solution.py:417
  65.7 0.5 copy-done.10
  66.2 0.0 copy-done.11
  66.3 0.2 copy-done.8
  66.4 0.1 copy-done.9
  66.5 10.5 %scales.1 = (f32[8,192,128]{2,1,0:T(8,128)}, bf16[8,192,128]{2,1,0:T(8,128)(2,1)}, bf16[8,192,128]{2,1,0:T(8,128)(2,1)}, f32[32,128]{1,0:T(8,128)}) custom-call(s32[2,8,4]{2,1,0:T(8,128)} %subtract_clamp_fusion.pos_ref, bf16[8,8,24,128]{3,2,1,0:T(8,128)(2,1)} %copy-done.8, bf16[8,8,24,128]{3,2,1,0:T(8,128)(2,1)} %copy-done, ...), custom_call_target="tpu_custom_call" | custom-call | flops 2000000000 | bytes 8000000 | tf_op jit(solution)/shard_map/scales/pallas_call | solution.py:434
  77.0 1.3 %collective-permute-start.4 = (bf16[8,192,128]{2,1,0:T(8,128)(2,1)}, bf16[8,192,128]{2,1,0:T(8,128)(2,1)S(1)}, u32[]{:S(2)}, u32[]{:S(2)}) collective-permute-start(bf16[8,192,128]{2,1,0:T(8,128)(2,1)} %get-tuple-element.26), channel_id=1, source_target_pairs={{1,0},{2,1},{3,2},{5,4},{6,5},{7,6},{9,8},{10,9},{11,10},{13,12},{... | collective-permute-start | bytes 1179656 | tf_op jit(solution)/shard_map/ppermute | solution.py:457
  78.3 4.9 %collective-permute-start.5 = (bf16[8,192,128]{2,1,0:T(8,128)(2,1)}, bf16[8,192,128]{2,1,0:T(8,128)(2,1)S(1)}, u32[]{:S(2)}, u32[]{:S(2)}) collective-permute-start(bf16[8,192,128]{2,1,0:T(8,128)(2,1)} %get-tuple-element.27), channel_id=1, source_target_pairs={{0,1},{1,2},{2,3},{4,5},{5,6},{6,7},{8,9},{9,10},{10,11},{12,13},{... | collective-permute-start | bytes 1179656 | tf_op jit(solution)/shard_map/ppermute | solution.py:458
  83.2 6.6 %all-to-all-start.3 = ((f32[32,1,128]{2,1,0:T(1,128)}), f32[32,1,128]{2,1,0:T(1,128)S(1)}, u32[]{:S(2)}, u32[]{:S(2)}) async-start(f32[32,1,128]{2,1,0:T(1,128)} %bitcast.8), calls=%async_computation.3 | async-start | bytes 32768 | tf_op jit(solution)/shard_map/all_to_all | solution.py:469
  89.8 0.0 copy-start.3
  89.9 0.7 copy-done.3
  90.6 0.1 copy-done.4
  90.7 2.2 %join.1 = bf16[8,8,24,128]{3,2,1,0:T(8,128)(2,1)} custom-call(f32[8,192,128]{2,1,0:T(8,128)} %get-tuple-element.25.center_ref, bf16[8,192,128]{2,1,0:T(8,128)(2,1)} %copy-done.3, bf16[8,192,128]{2,1,0:T(8,128)(2,1)} %copy-done.4), custom_call_target="tpu_custom_call" | custom-call | flops 1000000 | bytes 2000000 | tf_op jit(solution)/shard_map/join/pallas_call | solution.py:459
  92.9 4.0 %all-to-all-done.3 = f32[32,1,128]{2,1,0:T(1,128)S(1)} async-done(((f32[32,1,128]{2,1,0:T(1,128)}), f32[32,1,128]{2,1,0:T(1,128)S(1)}, u32[]{:S(2)}, u32[]{:S(2)}) %all-to-all-start.3) | async-done | bytes 16416 | tf_op jit(solution)/shard_map/all_to_all | solution.py:469
  97.0 3.5 %all-to-all-start.2 = ((bf16[8,8,24,128]{3,2,1,0:T(8,128)(2,1)}), bf16[8,8,24,128]{3,2,1,0:T(8,128)(2,1)S(1)}, u32[]{:S(2)}, u32[]{:S(2)}) async-start(bf16[8,8,24,128]{3,2,1,0:T(8,128)(2,1)} %join.1), calls=%async_computation.2 | async-start | bytes 786432 | tf_op jit(solution)/shard_map/all_to_all | solution.py:468
  100.5 0.6 slice_reduce_fusion
  101.7 10.7 %all-to-all-done.2.g_ref = bf16[8,8,24,128]{3,2,1,0:T(8,128)(2,1)S(1)} async-done(((bf16[8,8,24,128]{3,2,1,0:T(8,128)(2,1)}), bf16[8,8,24,128]{3,2,1,0:T(8,128)(2,1)S(1)}, u32[]{:S(2)}, u32[]{:S(2)}) %all-to-all-start.2) | async-done | bytes 393248 | tf_op jit(solution)/shard_map/all_to_all | solution.py:468
  112.4 0.8 copy-done.2
  113.1 9.6 %bwd.1 = bf16[2,1024,1024]{2,1,0:T(8,128)(2,1)} custom-call(bf16[8,8,24,128]{3,2,1,0:T(8,128)(2,1)} %copy-done.2, bf16[2,192,1024]{2,1,0:T(8,128)(2,1)} %get-tuple-element.28.at_ref, bf16[2,1024,1024]{2,1,0:T(8,128)(2,1)} %get-tuple-element.29.slope_ref, bf16[1024,1024]{1,0:T(8,128)(2,1)} %get-tuple-element.30.w_int_ref), custom_call_target="tpu_custom_call" | custom-call | flops 4294967296 | bytes 12000000 | tf_op jit(solution)/shard_map/bwd/pallas_call | solution.py:472
  (23 shorter events, 0.1 us)
Async XLA Ops:
  2.4 34.6 %copy-start.5 = (f32[12,1024]{1,0:T(8,128)S(1)}, f32[12,1024]{1,0:T(8,128)}, u32[]{:S(2)}) copy-start(f32[12,1024]{1,0:T(8,128)} %param.18) | copy-start | bytes 147460
  2.4 37.9 %copy-start.7 = (s32[2,8,4]{1,2,0:T(4,128)S(1)}, s32[2,8,4]{1,2,0:T(4,128)}, u32[]{:S(2)}) copy-start(s32[2,8,4]{1,2,0:T(4,128)} %param.22) | copy-start | bytes 772
  33.6 26.3 %copy-start = (bf16[8,8,24,128]{3,2,1,0:T(8,128)(2,1)}, bf16[8,8,24,128]{3,2,1,0:T(8,128)(2,1)S(1)}, u32[]{:S(2)}) copy-start(bf16[8,8,24,128]{3,2,1,0:T(8,128)(2,1)S(1)} %all_to_all.27.hi_ref.own_ref) | copy-start | bytes 1179652
  33.6 26.9 %all-to-all-start.1 = ((bf16[8,8,24,128]{3,2,1,0:T(8,128)(2,1)}), bf16[8,8,24,128]{3,2,1,0:T(8,128)(2,1)S(1)}, u32[]{:S(2)}, u32[]{:S(2)}) async-start(bf16[8,8,24,128]{3,2,1,0:T(8,128)(2,1)} %get-tuple-element.21), calls=%async_computation.1 | async-start | bytes 786432 | tf_op jit(solution)/shard_map/all_to_all | solution.py:371
  37.1 22.8 %copy-start.6 = (bf16[16,1024]{1,0:T(8,128)(2,1)}, bf16[16,1024]{1,0:T(8,128)(2,1)S(1)}, u32[]{:S(2)}) copy-start(bf16[16,1024]{1,0:T(8,128)(2,1)S(1)} %pad.6.to_ref) | copy-start | bytes 98308
  37.1 28.5 %collective-permute-start.2 = (bf16[16,1024]{1,0:T(8,128)(2,1)S(1)}, bf16[16,1024]{1,0:T(8,128)(2,1)S(1)}, u32[]{:S(2)}, u32[]{:S(2)}) collective-permute-start(bf16[16,1024]{1,0:T(8,128)(2,1)S(1)} %pad.6.to_ref), channel_id=1, source_target_pairs={{0,1},{1,2},{2,3},{4,5},{5,6},{6,7},{8,9},{9,10},{10,11},{12,13},{... | collective-permute-start | bytes 98312 | tf_op jit(solution)/shard_map/ppermute | solution.py:410
  38.4 27.2 %collective-permute-start.3 = (bf16[16,1024]{1,0:T(8,128)(2,1)S(1)}, bf16[16,1024]{1,0:T(8,128)(2,1)S(1)}, u32[]{:S(2)}, u32[]{:S(2)}) collective-permute-start(bf16[16,1024]{1,0:T(8,128)(2,1)S(1)} %pad.6.to_ref), channel_id=1, source_target_pairs={{1,0},{2,1},{3,2},{5,4},{6,5},{7,6},{9,8},{10,9},{11,10},{13,12},{... | collective-permute-start | bytes 98312 | tf_op jit(solution)/shard_map/ppermute | solution.py:411
  40.4 25.2 %collective-permute-start = (bf16[8,8,24,128]{3,2,1,0:T(8,128)(2,1)S(1)}, bf16[8,8,24,128]{3,2,1,0:T(8,128)(2,1)S(1)}, u32[]{:S(2)}, u32[]{:S(2)}) collective-permute-start(bf16[8,8,24,128]{3,2,1,0:T(8,128)(2,1)S(1)} %all_to_all.27.hi_ref.own_ref), channel_id=1, source_target_pairs={{0,1},{1,2},{2,3},{4,5},{5,6},{6,7},{8,9},{9,10},{10,11},{12,13},{... | collective-permute-start | bytes 1179656 | tf_op jit(solution)/shard_map/ppermute | solution.py:412
  45.2 20.5 %collective-permute-start.1 = (bf16[8,8,24,128]{3,2,1,0:T(8,128)(2,1)S(1)}, bf16[8,8,24,128]{3,2,1,0:T(8,128)(2,1)S(1)}, u32[]{:S(2)}, u32[]{:S(2)}) collective-permute-start(bf16[8,8,24,128]{3,2,1,0:T(8,128)(2,1)S(1)} %all_to_all.27.hi_ref.own_ref), channel_id=1, source_target_pairs={{1,0},{2,1},{3,2},{5,4},{6,5},{7,6},{9,8},{10,9},{11,10},{13,12},{... | collective-permute-start | bytes 1179656 | tf_op jit(solution)/shard_map/ppermute | solution.py:413
  60.5 0.7 copy-start.1
  65.6 0.6 copy-start.10
  65.6 0.6 copy-start.11
  65.7 0.8 copy-start.8
  65.7 0.9 copy-start.9
  77.0 12.8 %collective-permute-start.4 = (bf16[8,192,128]{2,1,0:T(8,128)(2,1)}, bf16[8,192,128]{2,1,0:T(8,128)(2,1)S(1)}, u32[]{:S(2)}, u32[]{:S(2)}) collective-permute-start(bf16[8,192,128]{2,1,0:T(8,128)(2,1)} %get-tuple-element.26), channel_id=1, source_target_pairs={{1,0},{2,1},{3,2},{5,4},{6,5},{7,6},{9,8},{10,9},{11,10},{13,12},{... | collective-permute-start | bytes 1179656 | tf_op jit(solution)/shard_map/ppermute | solution.py:457
  78.3 11.5 %collective-permute-start.5 = (bf16[8,192,128]{2,1,0:T(8,128)(2,1)}, bf16[8,192,128]{2,1,0:T(8,128)(2,1)S(1)}, u32[]{:S(2)}, u32[]{:S(2)}) collective-permute-start(bf16[8,192,128]{2,1,0:T(8,128)(2,1)} %get-tuple-element.27), channel_id=1, source_target_pairs={{0,1},{1,2},{2,3},{4,5},{5,6},{6,7},{8,9},{9,10},{10,11},{12,13},{... | collective-permute-start | bytes 1179656 | tf_op jit(solution)/shard_map/ppermute | solution.py:458
  83.2 13.8 %all-to-all-start.3 = ((f32[32,1,128]{2,1,0:T(1,128)}), f32[32,1,128]{2,1,0:T(1,128)S(1)}, u32[]{:S(2)}, u32[]{:S(2)}) async-start(f32[32,1,128]{2,1,0:T(1,128)} %bitcast.8), calls=%async_computation.3 | async-start | bytes 32768 | tf_op jit(solution)/shard_map/all_to_all | solution.py:469
  89.8 0.7 copy-start.3
  89.8 0.9 copy-start.4
  97.0 15.4 %all-to-all-start.2 = ((bf16[8,8,24,128]{3,2,1,0:T(8,128)(2,1)}), bf16[8,8,24,128]{3,2,1,0:T(8,128)(2,1)S(1)}, u32[]{:S(2)}, u32[]{:S(2)}) async-start(bf16[8,8,24,128]{3,2,1,0:T(8,128)(2,1)} %join.1), calls=%async_computation.2 | async-start | bytes 786432 | tf_op jit(solution)/shard_map/all_to_all | solution.py:468
  112.4 0.8 copy-start.2
where the time goes:
time: 125 us; the launch traced here: 124 us
  Pallas kernels  51.9 us (42%)
  starting transfers between devices  28.3 us (23%)
  blocking collectives  19.4 us (16%)
  waiting for transfers between devices  14.7 us (12%)
  local copies, waits for them, and re-layouts  5.77 us (5%)
  between operations  2.62 us (2%)
    all_to_all x1, blocking collectives, on_device(): lax.all_to_all(hi, 'member', split_axis=0, concat_axis=0, tiled=True)  19.4 us
    pallas_call x1, Pallas kernels, on_device(): pl.pallas_call(functools.partial(prep_kernel, lay, slots), grid=(prep_ste...  13.4 us
    pallas_call x1, Pallas kernels, on_device(): pl.pallas_call(functools.partial(fwd_kernel, lay), grid=(steps,), in_spec...  11.8 us
    all_to_all x1, waiting for transfers between devices, on_device(): lax.all_to_all(joined, 'member', split_axis=0, concat_axis=0, tiled=True)  10.7 us
    pallas_call x1, Pallas kernels, on_device(): pl.pallas_call(functools.partial(scales_kernel, lay, slots), in_specs=[SM...  10.5 us
    pallas_call x1, Pallas kernels, on_device(): pl.pallas_call(functools.partial(bwd_kernel, lay), grid=(steps,), in_spec...  9.57 us
    all_to_all x1, starting transfers between devices, on_device(): lax.all_to_all(losses, ('member', 'grid'), split_axis=0, concat_axis=0, t...  6.57 us
    unnamed x26, local copies, waits for them, and re-layouts  5.12 us
  transfers between devices with their start and end apart: 9, of which 2 were waited for; matrix products, arithmetic and copies ran while one was open for 2% of the time, Pallas kernels for 16%

commit v1 on v0

v1 whole, which is shorter than its diff:
```python
import functools
import math

import jax
import jax.numpy as jnp
import numpy as np
from jax import lax
from jax.experimental import pallas as pl
from jax.experimental.pallas import tpu as pltpu
from jax.sharding import PartitionSpec as P

kernel_eps = 0.01
f32 = jnp.float32
bf16 = jnp.bfloat16
SUB = 8
GELU_C = math.sqrt(2.0 / math.pi)
GELU_A = 0.044715


class Layout:
    def __init__(self, senders, own_members, variables, blocks, block):
        self.senders = senders
        self.own = own_members
        self.vars = variables
        self.blocks = blocks
        self.block = block
        rest = variables % SUB
        self.half = 0 < rest <= SUB // 2 and own_members % 2 == 0 and blocks % 2 == 0
        self.whole = variables // SUB if self.half or rest == 0 else variables // SUB + 1
        self.piece = own_members * (self.whole * SUB + (SUB // 2 if self.half else 0))
        self.rows = senders * self.piece
        self.members = senders * own_members
        self.tiles = blocks * self.whole + (blocks // 2 if self.half else 0)
        self.truth_rows = -(-variables // 16) * 16
        self.total_rows = self.rows + self.truth_rows

    def permutation(self):
        out = np.zeros((self.own, self.senders * self.vars, self.rows), np.float32)
        for sender in range(self.senders):
            for c in range(self.piece):
                if c < self.whole * self.own * SUB:
                    v = c // (self.own * SUB) * SUB + c % SUB
                    m = c // SUB % self.own
                else:
                    tail = c - self.whole * self.own * SUB
                    v = self.whole * SUB + tail % (SUB // 2)
                    m = tail // (SUB // 2)
                if v < self.vars:
                    out[m, sender * self.vars + v, sender * self.piece + c] = 1.0
        return out


def low_half():
    return lax.broadcasted_iota(jnp.int32, (SUB, 128), 0) < SUB // 2


def swap(x):
    return pltpu.roll(x, SUB // 2, 0)


def rows_to_tiles(lay, take, put, put_truth):
    step = 2 if lay.half else 1
    for r0 in range(0, lay.blocks, step):
        rows = [take(r0 + d) for d in range(step)]
        for d in range(step):
            for a in range(lay.whole):
                t = (r0 + d) * lay.whole + a
                for sender in range(lay.senders):
                    for m in range(lay.own):
                        at = sender * lay.piece + (a * lay.own + m) * SUB
                        put(t, sender * lay.own + m, rows[d][at : at + SUB])
                at = lay.rows + a * SUB
                put_truth(t, rows[d][at : at + SUB])
        if lay.half:
            t = lay.blocks * lay.whole + r0 // 2
            low = low_half()
            for sender in range(lay.senders):
                for m in range(0, lay.own, 2):
                    at = sender * lay.piece + lay.whole * lay.own * SUB + m * (SUB // 2)
                    first, second = rows[0][at : at + SUB], rows[1][at : at + SUB]
                    put(t, sender * lay.own + m, jnp.where(low, first, swap(second)))
                    put(t, sender * lay.own + m + 1, jnp.where(low, swap(first), second))
            at = lay.rows + lay.whole * SUB
            first, second = rows[0][at : at + SUB], rows[1][at : at + SUB]
            put_truth(t, jnp.where(low, first, swap(second)))


def tiles_to_rows(lay, get, put):
    for r in range(lay.blocks):
        for sender in range(lay.senders):
            for a in range(lay.whole):
                for m in range(lay.own):
                    at = sender * lay.piece + (a * lay.own + m) * SUB
                    put(r, at, get(r * lay.whole + a, sender * lay.own + m))
            if lay.half:
                t = lay.blocks * lay.whole + r // 2
                low = low_half()
                for m in range(0, lay.own, 2):
                    at = sender * lay.piece + lay.whole * lay.own * SUB + m * (SUB // 2)
                    first = get(t, sender * lay.own + m)
                    second = get(t, sender * lay.own + m + 1)
                    if r % 2 == 0:
                        put(r, at, jnp.where(low, first, swap(second)))
                    else:
                        put(r, at, jnp.where(low, swap(first), second))


def crps_tile(x, y, w):
    members = len(x)
    inv_total = None
    pulls = [None] * members
    for i in range(members):
        for j in range(i + 1, members):
            d = x[i] - x[j]
            inv = lax.rsqrt(d * d + kernel_eps)
            dk = d * inv
            inv_total = inv if inv_total is None else inv_total + inv
            pulls[i] = dk if pulls[i] is None else pulls[i] + dk
            pulls[j] = -dk if pulls[j] is None else pulls[j] - dk
    pair_total = kernel_eps * inv_total
    miss_total = None
    grads = []
    for i in range(members):
        d = x[i] - y
        t = d * d + kernel_eps
        inv = lax.rsqrt(t)
        k = t * inv
        miss_total = k if miss_total is None else miss_total + k
        pair_total = pair_total + d * pulls[i]
        grads.append(w * (d * inv - pulls[i] * (1.0 / (members - 1))))
    score = miss_total * (1.0 / members) - pair_total * (1.0 / (members * (members - 1)))
    return w * score, grads


def crps_loop(lay, x_ref, y_ref, w_ref, total_ref):
    def step(t, total):
        x = [x_ref[t, m] for m in range(lay.members)]
        part, grads = crps_tile(x, y_ref[t], w_ref[t])
        for m in range(lay.members):
            x_ref[t, m] = grads[m]
        return total + part

    total_ref[...] = lax.fori_loop(0, lay.tiles, step, total_ref[...])


CHUNK = 256
NT = (((1,), (1,)), ((), ()))


def fwd_kernel(lay, lat_ref, w_in_ref, b_in_ref, w_out_ref, perm_ref, b_out_ref, hi_ref, lo_ref, pre_ref, a_ref, bias_scr):
    @pl.when(pl.program_id(0) == 0)
    def _():
        spread = None
        for m in range(lay.own):
            p = perm_ref[m]
            a_ref[m] = jnp.dot(p, w_out_ref[...], preferred_element_type=f32).astype(bf16)
            spread = p.astype(f32) if spread is None else spread + p.astype(f32)
        bias = jnp.broadcast_to(b_out_ref[...], (lay.block, b_out_ref.shape[1]))
        bias_scr[...] = lax.dot_general(
            spread, bias, NT, precision=lax.Precision.HIGHEST, preferred_element_type=f32
        )

    tile = lat_ref.shape[1]
    lat = lat_ref[...].reshape(lay.own * tile, lat_ref.shape[2])
    field = None
    for c in range(0, w_in_ref.shape[1], CHUNK):
        cols = slice(c, c + CHUNK)
        pre = jnp.dot(lat, w_in_ref[:, cols], preferred_element_type=f32) + b_in_ref[:, cols]
        inner = pre * (GELU_C + (GELU_C * GELU_A) * (pre * pre))
        half = 0.5 * pre
        hidden = (half + half * jnp.tanh(inner)).astype(bf16)
        for m in range(lay.own):
            rows = slice(m * tile, (m + 1) * tile)
            pre_ref[m, :, cols] = pre[rows].astype(bf16)
            part = lax.dot_general(a_ref[m, :, cols], hidden[rows], NT, preferred_element_type=f32)
            field = part if field is None else field + part
    for r in range(hi_ref.shape[1]):
        block = field[:, r * lay.block : (r + 1) * lay.block] + bias_scr[...]
        for sender in range(lay.senders):
            part = block[sender * lay.piece : (sender + 1) * lay.piece]
            hi = part.astype(bf16)
            hi_ref[sender, r] = hi
            lo_ref[sender, r] = (part - hi.astype(f32)).astype(bf16)


SLAB = 16


def prep_kernel(lay, slots, vw_ref, count_ref, pre_ref, sm_ref, area_ref, slope_ref, wb_ref, w_ref):
    step = pl.program_id(0)
    rows = pre_ref.shape[1]

    @pl.when(step == 0)
    def _():
        kind = lax.broadcasted_iota(jnp.int32, (lay.truth_rows, lay.block), 0)
        column = jnp.zeros((lay.truth_rows, lay.block), f32)
        for v in range(lay.vars):
            column = jnp.where(kind == v, vw_ref[v], column)

        def weights(r):
            return column * area_ref[:, r * lay.block : (r + 1) * lay.block]

        for r in range(lay.blocks):
            w = weights(r)
            for a in range(lay.whole):
                w_ref[r * lay.whole + a] = w[a * SUB : (a + 1) * SUB]
            if lay.half and r % 2:
                at = lay.whole * SUB
                first, second = weights(r - 1)[at : at + SUB], w[at : at + SUB]
                w_ref[lay.blocks * lay.whole + r // 2] = jnp.where(low_half(), first, swap(second))

    for m in range(lay.own):

        def slab(i, carry):
            at = pl.ds(pl.multiple_of(i * SLAB, SLAB), SLAB)
            x = pre_ref[m, at, :].astype(f32)
            p = GELU_C + (GELU_C * GELU_A) * (x * x)
            up = 0.5 + 0.5 * jnp.tanh(x * p)
            bend = (x * (6.0 * p - 4.0 * GELU_C)) * (1.0 - up)
            slope_ref[m, at, :] = (up + up * bend).astype(bf16)
            return carry

        lax.fori_loop(0, rows // SLAB, slab, 0)

    for s in range(sm_ref.shape[0]):
        for k in range(slots):
            live = (k < count_ref[s, step]).astype(f32)
            wb_ref[s, 0, k * lay.block : (k + 1) * lay.block, :] = (sm_ref[s, 0, k] * live).astype(bf16)


def pack_kernel(lay, field_ref, target_ref, out_ref):
    for r in range(lay.blocks):
        field = field_ref[:, r].astype(f32).reshape(lay.rows, lay.block)
        truth = target_ref[:, r * lay.block : (r + 1) * lay.block]
        fill = jnp.zeros((lay.truth_rows - lay.vars, lay.block), f32)
        out_ref[r, : lay.rows] = field.astype(bf16)
        out_ref[r, lay.rows :] = jnp.concatenate([truth, fill], 0).astype(bf16)


def raw_kernel(lay, hi_ref, lo_ref, target_ref, w_ref, grad_ref, total_ref, x_scr, y_scr):
    def take(r):
        field = hi_ref[:, r].astype(f32) + lo_ref[:, r].astype(f32)
        truth = target_ref[:, r * lay.block : (r + 1) * lay.block]
        fill = jnp.zeros((lay.truth_rows - lay.vars, lay.block), f32)
        return jnp.concatenate([field.reshape(lay.rows, lay.block), truth, fill], 0)

    def put(t, m, tile):
        x_scr[t, m] = tile

    def put_truth(t, tile):
        y_scr[t] = tile

    rows_to_tiles(lay, take, put, put_truth)
    total_ref[...] = jnp.zeros_like(total_ref)
    crps_loop(lay, x_scr, y_scr, w_ref, total_ref)

    def put_rows(r, at, tile):
        grad_ref[r, at : at + SUB] = tile

    tiles_to_rows(lay, lambda t, m: x_scr[t, m], put_rows)


def scales_kernel(lay, slots, pos_ref, own_ref, inner_ref, outer_ref, wb_ref, w_ref, center_ref, to_inner_ref, to_outer_ref, total_ref, ext_scr, x_scr, y_scr, row_scr, adj_scr):
    scales = wb_ref.shape[0]
    block = lay.block
    n = lay.blocks
    for at, src in enumerate((own_ref, inner_ref, outer_ref)):
        ext_scr[at * n : (at + 1) * n] = src[...]
    total_ref[...] = jnp.zeros_like(total_ref)
    adj_scr[...] = jnp.zeros_like(adj_scr)
    for s in range(scales):

        def take(r):
            gathered = jnp.concatenate([ext_scr[pos_ref[s, r, k]] for k in range(slots)], 1)
            return jnp.dot(gathered, wb_ref[s, r], preferred_element_type=f32)

        def put(t, m, tile):
            x_scr[t, m] = tile

        def put_truth(t, tile):
            y_scr[t] = tile

        rows_to_tiles(lay, take, put, put_truth)
        crps_loop(lay, x_scr, y_scr, w_ref, total_ref)

        def put_rows(r, at, tile):
            row_scr[r, at : at + SUB] = tile

        tiles_to_rows(lay, lambda t, m: x_scr[t, m], put_rows)
        for r in range(n):
            back = lax.dot_general(row_scr[r].astype(bf16), wb_ref[s, r], NT, preferred_element_type=f32)
            for k in range(slots):
                p = pos_ref[s, r, k]
                adj_scr[p] = adj_scr[p] + back[:, k * block : (k + 1) * block]
    center_ref[...] = adj_scr[0:n]
    to_inner_ref[...] = adj_scr[n : 2 * n].astype(bf16)
    to_outer_ref[...] = adj_scr[2 * n : 3 * n].astype(bf16)


LOSS_ROWS = 16


def join_kernel(lay, center_ref, base_ref, a_ref, b_ref, ta_ref, tb_ref, out_ref):
    total = jnp.broadcast_to(jnp.sum(ta_ref[...] + tb_ref[...]), (LOSS_ROWS, lay.block))
    high = total.astype(bf16).astype(f32)
    mid = (total - high).astype(bf16).astype(f32)
    kind = lax.broadcasted_iota(jnp.int32, (LOSS_ROWS, lay.block), 0)
    tail = jnp.where(kind == 0, high, jnp.where(kind == 1, mid, jnp.where(kind == 2, total - high - mid, 0.0)))
    for sender in range(lay.senders):
        rows = slice(sender * lay.piece, (sender + 1) * lay.piece)
        parts = []
        for r in range(lay.blocks):
            local = center_ref[r, rows] + base_ref[r, rows]
            parts.append(local + (a_ref[r, rows].astype(f32) + b_ref[r, rows].astype(f32)))
        out_ref[sender] = jnp.concatenate(parts + [tail], 0).astype(bf16)


def bwd_kernel(lay, g_ref, a_ref, slope_ref, w_in_ref, out_ref):
    tile = out_ref.shape[1]
    count = tile // lay.block
    span = count * lay.piece
    at = pl.ds(pl.multiple_of(pl.program_id(0) * span, 16), span)
    g = g_ref[:, at, :].astype(f32)
    cols = []
    for r in range(count):
        rows = g[:, r * lay.piece : (r + 1) * lay.piece].reshape(lay.rows, lay.block)
        cols.append(rows.T.astype(bf16))
    grads = jnp.concatenate(cols, 0)
    parts = []
    for m in range(lay.own):
        hidden_grad = jnp.dot(grads, a_ref[m], preferred_element_type=f32)
        parts.append((hidden_grad * slope_ref[m].astype(f32)).astype(bf16))
    pre_grad = jnp.concatenate(parts, 0)
    for c in range(0, w_in_ref.shape[0], CHUNK):
        cols = slice(c, c + CHUNK)
        part = lax.dot_general(pre_grad, w_in_ref[cols, :], NT, preferred_element_type=f32).astype(bf16)
        for m in range(lay.own):
            out_ref[m, :, cols] = part[m * tile : (m + 1) * tile]


def params(mib):
    return pltpu.CompilerParams(vmem_limit_bytes=mib * 1024 * 1024)


def cost(flops, nbytes, trans=0):
    return pl.CostEstimate(flops=int(flops), bytes_accessed=int(nbytes), transcendentals=int(trans))


VM = pl.BlockSpec(memory_space=pltpu.VMEM)
SM = pl.BlockSpec(memory_space=pltpu.SMEM)


def whole_spec(shape):
    return pl.BlockSpec(shape, lambda i: (0,) * len(shape))


def exchange(block, axis):
    n = lax.axis_size(axis)
    out = []
    for first in (0, 1):
        route = []
        for i in range(first, n - 1, 2):
            route += [(i, i + 1), (i + 1, i)]
        out.append(lax.ppermute(block[first] if isinstance(block, tuple) else block, axis, route))
    return out


def on_device(
    latents,
    w_in,
    b_in,
    w_out,
    b_out,
    target,
    area_weight,
    var_weight,
    smoothers,
    block_index,
    block_count,
):
    own, points, width = latents.shape
    hidden_width = w_in.shape[1]
    var_total = w_out.shape[1]
    var_local = target.shape[0]
    scales, blocks, slots, block, _ = smoothers.shape
    senders = lax.axis_size("member")
    devices_grid = lax.axis_size("grid")
    lay = Layout(senders, own, var_local, blocks, block)
    perm = jnp.asarray(lay.permutation().transpose(0, 2, 1), bf16)
    payload = (senders, blocks, lay.piece, block)

    tile = min(points, 256)
    steps = points // tile
    tile_blocks = tile // block
    payload_spec = pl.BlockSpec((senders, tile_blocks, lay.piece, block), lambda i: (0, i, 0, 0))
    wide_spec = pl.BlockSpec((own, tile, hidden_width), lambda i: (0, i, 0))
    a_shape = (own, lay.rows, hidden_width)
    hi, lo, pre, spread_out = pl.pallas_call(
        functools.partial(fwd_kernel, lay),
        grid=(steps,),
        in_specs=[
            pl.BlockSpec((own, tile, width), lambda i: (0, i, 0)),
            whole_spec(w_in.shape),
            whole_spec((1, hidden_width)),
            whole_spec((var_total, hidden_width)),
            whole_spec(perm.shape),
            whole_spec((1, var_total)),
        ],
        out_specs=[payload_spec, payload_spec, wide_spec, whole_spec(a_shape)],
        out_shape=[
            jax.ShapeDtypeStruct(payload, bf16),
            jax.ShapeDtypeStruct(payload, bf16),
            jax.ShapeDtypeStruct((own, points, hidden_width), bf16),
            jax.ShapeDtypeStruct(a_shape, bf16),
        ],
        scratch_shapes=[pltpu.VMEM((lay.rows, lay.block), f32)],
        compiler_params=params(60),
        cost_estimate=cost(2 * own * points * width * hidden_width, 12e6, own * points * hidden_width),
        name="fwd",
    )(latents, w_in, b_in.reshape(1, -1), w_out.T, perm, b_out.reshape(1, -1))

    with jax.named_scope("hi"):
        own_hi = lax.all_to_all(hi, "member", split_axis=0, concat_axis=0, tiled=True)

    grad_shape = (blocks, lay.rows, block)
    tile_shape = (lay.tiles, lay.members, SUB, block)
    prep_tile = points // blocks
    with jax.named_scope("prep"):
        slope, wb, w_tiles = pl.pallas_call(
            functools.partial(prep_kernel, lay, slots),
            grid=(blocks,),
            in_specs=[
                SM,
                SM,
                pl.BlockSpec((own, prep_tile, hidden_width), lambda i: (0, i, 0)),
                pl.BlockSpec((scales, 1, slots, block, block), lambda i: (0, i, 0, 0, 0)),
                whole_spec((1, points)),
            ],
            out_specs=[
                pl.BlockSpec((own, prep_tile, hidden_width), lambda i: (0, i, 0)),
                pl.BlockSpec((scales, 1, slots * block, block), lambda i: (0, i, 0, 0)),
                whole_spec((lay.tiles, SUB, block)),
            ],
            out_shape=[
                jax.ShapeDtypeStruct((own, points, hidden_width), bf16),
                jax.ShapeDtypeStruct((scales, blocks, slots * block, block), bf16),
                jax.ShapeDtypeStruct((lay.tiles, SUB, block), f32),
            ],
            compiler_params=params(57),
            cost_estimate=cost(1e8, 1.4e7, own * points * hidden_width),
            name="prep",
        )(var_weight, block_count, pre, smoothers, area_weight.reshape(1, -1))
        rank = lax.axis_index("grid")
        offset = block_index - rank * blocks
        odd = rank % 2
        lower_part, upper_part = 2 - odd, 1 + odd
        part = jnp.where(offset < 0, lower_part, jnp.where(offset >= blocks, upper_part, 0))
        positions = jnp.clip(part * blocks + offset % blocks, 0, 3 * blocks - 1)
        _, own_hi = lax.optimization_barrier((wb, own_hi))

    with jax.named_scope("pack"):
        joint = pl.pallas_call(
            functools.partial(pack_kernel, lay),
            in_specs=[VM, VM],
            out_specs=VM,
            out_shape=jax.ShapeDtypeStruct((blocks, lay.total_rows, block), bf16),
            compiler_params=params(8),
            cost_estimate=cost(1e6, 1e6),
            name="pack",
        )(own_hi, target)
    with jax.named_scope("halo"):
        inner, outer = exchange(joint, "grid")
    _, lo = lax.optimization_barrier((joint, lo))
    with jax.named_scope("lo"):
        own_lo = lax.all_to_all(lo, "member", split_axis=0, concat_axis=0, tiled=True)

    center, to_inner, to_outer, total = pl.pallas_call(
        functools.partial(scales_kernel, lay, slots),
        in_specs=[SM] + [VM] * 5,
        out_specs=[VM] * 4,
        out_shape=[
            jax.ShapeDtypeStruct(grad_shape, f32),
            jax.ShapeDtypeStruct(grad_shape, bf16),
            jax.ShapeDtypeStruct(grad_shape, bf16),
            jax.ShapeDtypeStruct((SUB, block), f32),
        ],
        scratch_shapes=[
            pltpu.VMEM((3 * blocks, lay.total_rows, block), bf16),
            pltpu.VMEM(tile_shape, f32),
            pltpu.VMEM((lay.tiles, SUB, block), f32),
            pltpu.VMEM(grad_shape, f32),
            pltpu.VMEM((3 * blocks, lay.rows, block), f32),
        ],
        compiler_params=params(16),
        cost_estimate=cost(2e9, 8e6, 4e6),
        name="scales",
    )(positions, joint, inner, outer, wb, w_tiles)

    with jax.named_scope("rims"):
        from_inner, from_outer = exchange((to_inner, to_outer), "grid")
    with jax.named_scope("raw"):
        _, own_lo = lax.optimization_barrier((total, own_lo))
        base, total_raw = pl.pallas_call(
            functools.partial(raw_kernel, lay),
            in_specs=[VM] * 4,
            out_specs=[VM, VM],
            out_shape=[
                jax.ShapeDtypeStruct(grad_shape, f32),
                jax.ShapeDtypeStruct((SUB, block), f32),
            ],
            scratch_shapes=[pltpu.VMEM(tile_shape, f32), pltpu.VMEM((lay.tiles, SUB, block), f32)],
            compiler_params=params(8),
            cost_estimate=cost(5e8, 3e6, 2e6),
            name="raw",
        )(own_hi, own_lo, target, w_tiles)

    joined = pl.pallas_call(
        functools.partial(join_kernel, lay),
        in_specs=[VM] * 6,
        out_specs=VM,
        out_shape=jax.ShapeDtypeStruct((senders, blocks * lay.piece + LOSS_ROWS, block), bf16),
        compiler_params=params(8),
        cost_estimate=cost(1e6, 2e6),
        name="join",
    )(center, base, from_inner, from_outer, total, total_raw)
    with jax.named_scope("back"):
        field_grad = lax.all_to_all(joined, "member", split_axis=0, concat_axis=0, tiled=True)
    with jax.named_scope("loss"):
        head = blocks * lay.piece
        by_member = jnp.sum(field_grad[:, head : head + 3, :].astype(f32), (0, 1))
        by_member = jnp.broadcast_to(by_member[None, None, :], (devices_grid, 1, block))
        parts = lax.all_to_all(by_member, "grid", split_axis=0, concat_axis=0, tiled=True)
        loss = jnp.sum(parts[:, 0, 0]) / ((scales + 1) * var_total * points * devices_grid)

    grad = pl.pallas_call(
        functools.partial(bwd_kernel, lay),
        grid=(steps,),
        in_specs=[
            whole_spec(joined.shape),
            whole_spec(a_shape),
            wide_spec,
            whole_spec(w_in.shape),
        ],
        out_specs=pl.BlockSpec((own, tile, width), lambda i: (0, i, 0)),
        out_shape=jax.ShapeDtypeStruct((own, points, width), bf16),
        compiler_params=params(58),
        cost_estimate=cost(2 * own * points * width * hidden_width, 12e6),
        name="bwd",
    )(field_grad, spread_out, slope, w_in)
    return grad, loss


def solution(mesh):
    in_specs = (
        P("member", "grid", None),
        P(),
        P(),
        P(),
        P(),
        P("member", "grid"),
        P("grid"),
        P("member"),
        P(None, "grid", None, None, None),
        P(None, "grid", None),
        P(None, "grid"),
    )
    out_specs = (P("member", "grid", None), P())
    return jax.shard_map(
        on_device, mesh=mesh, in_specs=in_specs, out_specs=out_specs, check_vma=False
    )
```

time: 125 us -> 94.5 us (0.76)
  waiting for transfers between devices: 14.7 us -> 1.03 us
  Pallas kernels: 51.9 us -> 45.3 us
  blocking collectives: 19.4 us -> 15 us
  local copies, waits for them, and re-layouts: 5.77 us -> 3.14 us
  starting transfers between devices: 28.3 us -> 26 us
    all_to_all x2, waiting for transfers between devices: 14.7 us -> 0.91 us  [the longest x1 0.91 us: on_device(): lax.all_to_all(hi, 'member', split_axis=0, concat_axis=0, tiled=True)]
    ppermute x6 -> x4, starting transfers between devices: 14.8 us -> 4.65 us  [exchange(): lax.ppermute(block[first] if isinstance(block, tuple) else block, axis, r...]
    pallas_call x3 -> x4, Pallas kernels: 20 us -> 13.1 us  [the longest x1 10.7 us: on_device(): pl.pallas_call(functools.partial(prep_kernel, lay, slots), grid=(blocks,)...]
    all_to_all x2, starting transfers between devices: 10 us -> 16.1 us  [the longest x1 8.77 us: on_device(): lax.all_to_all(by_member, 'grid', split_axis=0, concat_axis=0, tiled=True)]
    all_to_all x1, blocking collectives: 19.4 us -> 15 us  [on_device(): lax.all_to_all(joined, 'member', split_axis=0, concat_axis=0, tiled=True)]
    unnamed x26 -> x13, local copies, waits for them, and re-layouts: 5.12 us -> 2.49 us
    pallas_call x1, Pallas kernels: 11.8 us -> 14.3 us  [on_device(): pl.pallas_call(functools.partial(fwd_kernel, lay), grid=(steps,), in_spec...]
    pallas_call x1, Pallas kernels: 10.5 us -> 8.28 us  [on_device(): pl.pallas_call(functools.partial(scales_kernel, lay, slots), in_specs=[SM...]
  transfers between devices with their start and end apart: 9 -> 7, of which waited for: 2 -> 2; matrix products, arithmetic and copies ran while one was open for 2% -> 0% of each run, Pallas kernels for 16% -> 33%
where the time goes in v1:
time: 94.5 us; the launch traced here: 93.6 us
  Pallas kernels  45.3 us (48%)
  starting transfers between devices  26 us (28%)
  blocking collectives  15 us (16%)
  local copies, waits for them, and re-layouts  3.14 us (3%)
  between operations  2.51 us (3%)
  waiting for transfers between devices  1.03 us (1%)
    all_to_all x1, blocking collectives, on_device(): lax.all_to_all(joined, 'member', split_axis=0, concat_axis=0, tiled=True)  15 us
    pallas_call x1, Pallas kernels, on_device(): pl.pallas_call(functools.partial(fwd_kernel, lay), grid=(steps,), in_spec...  14.3 us
    pallas_call x1, Pallas kernels, on_device(): pl.pallas_call(functools.partial(prep_kernel, lay, slots), grid=(blocks,)...  10.7 us
    pallas_call x1, Pallas kernels, on_device(): pl.pallas_call(functools.partial(bwd_kernel, lay), grid=(steps,), in_spec...  9.63 us
    all_to_all x1, starting transfers between devices, on_device(): lax.all_to_all(by_member, 'grid', split_axis=0, concat_axis=0, tiled=True)  8.77 us
    pallas_call x1, Pallas kernels, on_device(): pl.pallas_call(functools.partial(scales_kernel, lay, slots), in_specs=[SM...  8.28 us
    all_to_all x1, starting transfers between devices, on_device(): lax.all_to_all(hi, 'member', split_axis=0, concat_axis=0, tiled=True)  7.32 us
    all_to_all x1, starting transfers between devices, on_device(): lax.all_to_all(lo, 'member', split_axis=0, concat_axis=0, tiled=True)  5.22 us
  transfers between devices with their start and end apart: 7, of which 2 were waited for; matrix products, arithmetic and copies ran while one was open for 0% of the time, Pallas kernels for 33%

profile of v1, /device:TPU:0, one launch (start us, length us, event | category | flops | bytes accessed | tf_op | source)
XLA Modules:
  0.0 93.6 jit_solution(11487608169371549442)
XLA Ops:
  0.6 14.3 %fwd.1 = (bf16[8,8,24,128]{3,2,1,0:T(8,128)(2,1)}, bf16[8,8,24,128]{3,2,1,0:T(8,128)(2,1)}, bf16[2,1024,1024]{2,1,0:T(8,128)(2,1)}, bf16[2,192,1024]{2,1,0:T(8,128)(2,1)}) custom-call(bf16[2,1024,1024]{2,1,0:T(8,128)(2,1)} %lat_ref.1, bf16[1024,1024]{1,0:T(8,128)(2,1)} %w_in_ref.3, f32[1,1024]{1,0:T(1,128)} %bitcast.6, bf16[96,1024]{1,0:T(8,128)(2,1)} %bitcast.5, ...), custom_call_target="tpu_custom_call" | custom-call | flops 4294967296 | bytes 12000000 | tf_op jit(solution)/shard_map/fwd/pallas_call | solution.py:398
  14.9 7.3 %all-to-all-start = ((bf16[8,8,24,128]{3,2,1,0:T(8,128)(2,1)}), bf16[8,8,24,128]{3,2,1,0:T(8,128)(2,1)S(1)}, u32[]{:S(2)}, u32[]{:S(2)}) async-start(bf16[8,8,24,128]{3,2,1,0:T(8,128)(2,1)} %get-tuple-element.20), calls=%async_computation | async-start | bytes 786432 | tf_op jit(solution)/shard_map/hi/all_to_all | solution.py:423
  22.2 0.0 copy-start.5
  22.2 10.7 %prep.1 = (bf16[2,1024,1024]{2,1,0:T(8,128)(2,1)}, bf16[2,8,512,128]{3,2,1,0:T(8,128)(2,1)}, f32[12,8,128]{2,1,0:T(8,128)}) custom-call(f32[12]{0:T(128)} %vw_ref.1, s32[2,8]{1,0:T(2,128)} %count_ref.1, bf16[2,1024,1024]{2,1,0:T(8,128)(2,1)} %get-tuple-element.18.pre_ref, f32[2,8,4,128,128]{4,3,2,1,0:T(8,128)} %sm_ref.1, f32[1,1024]{1,0:T(1,128)} %bitcast.4), custom_call_target="tpu_custom_call" | custom-call | flops 100000000 | bytes 14000000 | tf_op jit(solution)/shard_map/prep/prep/pallas_call | solution.py:429
  33.0 0.9 all-to-all-done.field_ref.hi_ref
  33.9 0.0 copy-done
  33.9 0.1 pack.1.own_ref
  34.0 0.7 collective-permute-start.1
  34.7 2.9 %collective-permute-start = (bf16[8,208,128]{2,1,0:T(8,128)(2,1)S(1)}, bf16[8,208,128]{2,1,0:T(8,128)(2,1)S(1)}, u32[]{:S(2)}, u32[]{:S(2)}) collective-permute-start(bf16[8,208,128]{2,1,0:T(8,128)(2,1)S(1)} %pack.1.own_ref), channel_id=1, source_target_pairs={{0,1},{1,0},{2,3},{3,2},{4,5},{5,4},{6,7},{7,6},{8,9},{9,8},{10,11... | collective-permute-start | bytes 1277960 | tf_op jit(solution)/shard_map/halo/ppermute | solution.py:364
  37.6 0.0 copy-done.5
  37.6 0.1 copy.16
  37.7 5.2 %all-to-all-start.1 = ((bf16[8,8,24,128]{3,2,1,0:T(8,128)(2,1)}), bf16[8,8,24,128]{3,2,1,0:T(8,128)(2,1)S(1)}, u32[]{:S(2)}, u32[]{:S(2)}) async-start(bf16[8,8,24,128]{3,2,1,0:T(8,128)(2,1)} %get-tuple-element.26), calls=%async_computation.1 | async-start | bytes 786432 | tf_op jit(solution)/shard_map/lo/all_to_all | solution.py:475
  42.9 0.0 collective-permute-done.1.outer_ref
  42.9 0.0 collective-permute-done.inner_ref
  42.9 1.6 %copy-done.1 = bf16[2,8,512,128]{3,2,1,0:T(8,128)(2,1)S(1)} copy-done((bf16[2,8,512,128]{3,2,1,0:T(8,128)(2,1)S(1)}, bf16[2,8,512,128]{3,2,1,0:T(8,128)(2,1)}, u32[]{:S(2)}) %copy-start.1) | copy-done | bytes 2097176
  44.5 0.8 copy-done.2
  45.3 8.3 %scales.1 = (f32[8,192,128]{2,1,0:T(8,128)S(1)}, bf16[8,192,128]{2,1,0:T(8,128)(2,1)}, bf16[8,192,128]{2,1,0:T(8,128)(2,1)}, f32[8,128]{1,0:T(8,128)S(1)}) custom-call(s32[2,8,4]{2,1,0:T(8,128)S(1)} %fusion.3.pos_ref, bf16[8,208,128]{2,1,0:T(8,128)(2,1)S(1)} %pack.1.own_ref, bf16[8,208,128]{2,1,0:T(8,128)(2,1)S(1)} %collective-permute-done.inner_ref, ...), custom_call_target="tpu_custom_call" | custom-call | flops 2000000000 | bytes 8000000 | tf_op jit(solution)/shard_map/scales/pallas_call | solution.py:477
  53.6 0.4 collective-permute-start.2
  54.0 0.7 collective-permute-start.3
  54.6 0.1 all-to-all-done.1.lo_ref
  54.8 0.0 copy-done.3
  54.8 2.1 %raw.1 = (f32[8,192,128]{2,1,0:T(8,128)S(1)}, f32[8,128]{1,0:T(8,128)S(1)}) custom-call(bf16[8,8,24,128]{3,2,1,0:T(8,128)(2,1)S(1)} %all-to-all-done.field_ref.hi_ref, bf16[8,8,24,128]{3,2,1,0:T(8,128)(2,1)S(1)} %all-to-all-done.1.lo_ref, f32[12,1024]{1,0:T(8,128)S(1)} %copy-done, f32[12,8,128]{2,1,0:T(8,128)S(1)} %copy-done.3), custom_call_target="tpu_custom_call" | custom-call | flops 500000000 | bytes 3000000 | tf_op jit(solution)/shard_map/raw/raw/pallas_call | solution.py:503
  56.9 0.0 collective-permute-done.2.a_ref
  56.9 0.0 collective-permute-done.3.b_ref
  56.9 0.2 join.1
  57.1 15.0 %all_to_all.20.g_ref = bf16[8,208,128]{2,1,0:T(8,128)(2,1)S(1)} all-to-all(bf16[8,208,128]{2,1,0:T(8,128)(2,1)S(1)} %join.1), channel_id=1, replica_groups=mesh['member'=8,'grid'=4] {'member'}, dimensions={0} | all-to-all | bytes 851968 | tf_op jit(solution)/shard_map/back/all_to_all | solution.py:527
  72.2 0.7 broadcast_in_dim.18
  72.8 8.8 %all-to-all-start.3 = ((f32[4,1,128]{2,1,0:T(1,128)}), f32[4,1,128]{2,1,0:T(1,128)S(1)}, u32[]{:S(2)}, u32[]{:S(2)}) async-start(f32[4,1,128]{2,1,0:T(1,128)} %broadcast_in_dim.18), calls=%async_computation.3 | async-start | bytes 4096 | tf_op jit(solution)/shard_map/loss/all_to_all | solution.py:532
  81.6 0.0 copy-done.4
  81.6 9.6 %bwd.1 = bf16[2,1024,1024]{2,1,0:T(8,128)(2,1)} custom-call(bf16[8,208,128]{2,1,0:T(8,128)(2,1)} %copy-done.4, bf16[2,192,1024]{2,1,0:T(8,128)(2,1)} %get-tuple-element.32.a_ref, bf16[2,1024,1024]{2,1,0:T(8,128)(2,1)} %get-tuple-element.33.slope_ref, bf16[1024,1024]{1,0:T(8,128)(2,1)} %w_in_ref.3), custom_call_target="tpu_custom_call" | custom-call | flops 4294967296 | bytes 12000000 | tf_op jit(solution)/shard_map/bwd/pallas_call | solution.py:535
  91.2 0.0 all-to-all-done.3
  91.2 0.6 slice_reduce_fusion
  (7 shorter events, 0.0 us)
Async XLA Ops:
  14.9 19.0 %all-to-all-start = ((bf16[8,8,24,128]{3,2,1,0:T(8,128)(2,1)}), bf16[8,8,24,128]{3,2,1,0:T(8,128)(2,1)S(1)}, u32[]{:S(2)}, u32[]{:S(2)}) async-start(bf16[8,8,24,128]{3,2,1,0:T(8,128)(2,1)} %get-tuple-element.20), calls=%async_computation | async-start | bytes 786432 | tf_op jit(solution)/shard_map/hi/all_to_all | solution.py:423
  22.2 11.7 %copy-start = (f32[12,1024]{1,0:T(8,128)S(1)}, f32[12,1024]{1,0:T(8,128)}, u32[]{:S(2)}) copy-start(f32[12,1024]{1,0:T(8,128)} %target_ref.3) | copy-start | bytes 147460
  22.2 15.3 %copy-start.5 = (s32[2,8,4]{1,2,0:T(4,128)S(1)}, s32[2,8,4]{1,2,0:T(4,128)}, u32[]{:S(2)}) copy-start(s32[2,8,4]{1,2,0:T(4,128)} %param.21) | copy-start | bytes 772
  34.0 8.9 %collective-permute-start.1 = (bf16[8,208,128]{2,1,0:T(8,128)(2,1)S(1)}, bf16[8,208,128]{2,1,0:T(8,128)(2,1)S(1)}, u32[]{:S(2)}, u32[]{:S(2)}) collective-permute-start(bf16[8,208,128]{2,1,0:T(8,128)(2,1)S(1)} %pack.1.own_ref), channel_id=1, source_target_pairs={{1,2},{2,1},{5,6},{6,5},{9,10},{10,9},{13,14},{14,13},{17,18},{18,... | collective-permute-start | bytes 1277960 | tf_op jit(solution)/shard_map/halo/ppermute | solution.py:364
  34.7 8.2 %collective-permute-start = (bf16[8,208,128]{2,1,0:T(8,128)(2,1)S(1)}, bf16[8,208,128]{2,1,0:T(8,128)(2,1)S(1)}, u32[]{:S(2)}, u32[]{:S(2)}) collective-permute-start(bf16[8,208,128]{2,1,0:T(8,128)(2,1)S(1)} %pack.1.own_ref), channel_id=1, source_target_pairs={{0,1},{1,0},{2,3},{3,2},{4,5},{5,4},{6,7},{7,6},{8,9},{9,8},{10,11... | collective-permute-start | bytes 1277960 | tf_op jit(solution)/shard_map/halo/ppermute | solution.py:364
  37.7 17.1 %copy-start.3 = (f32[12,8,128]{2,1,0:T(8,128)S(1)}, f32[12,8,128]{2,1,0:T(8,128)}, u32[]{:S(2)}) copy-start(f32[12,8,128]{2,1,0:T(8,128)} %get-tuple-element.22.w_ref) | copy-start | bytes 147460
  37.7 17.1 %all-to-all-start.1 = ((bf16[8,8,24,128]{3,2,1,0:T(8,128)(2,1)}), bf16[8,8,24,128]{3,2,1,0:T(8,128)(2,1)S(1)}, u32[]{:S(2)}, u32[]{:S(2)}) async-start(bf16[8,8,24,128]{3,2,1,0:T(8,128)(2,1)} %get-tuple-element.26), calls=%async_computation.1 | async-start | bytes 786432 | tf_op jit(solution)/shard_map/lo/all_to_all | solution.py:475
  42.9 1.6 %copy-start.1 = (bf16[2,8,512,128]{3,2,1,0:T(8,128)(2,1)S(1)}, bf16[2,8,512,128]{3,2,1,0:T(8,128)(2,1)}, u32[]{:S(2)}) copy-start(bf16[2,8,512,128]{3,2,1,0:T(8,128)(2,1)} %get-tuple-element.19.wb_ref) | copy-start | bytes 6291460
  44.5 0.8 copy-start.2
  53.6 3.3 %collective-permute-start.2 = (bf16[8,192,128]{2,1,0:T(8,128)(2,1)}, bf16[8,192,128]{2,1,0:T(8,128)(2,1)S(1)}, u32[]{:S(2)}, u32[]{:S(2)}) collective-permute-start(bf16[8,192,128]{2,1,0:T(8,128)(2,1)} %get-tuple-element.29), channel_id=1, source_target_pairs={{0,1},{1,0},{2,3},{3,2},{4,5},{5,4},{6,7},{7,6},{8,9},{9,8},{10,11... | collective-permute-start | bytes 1179656 | tf_op jit(solution)/shard_map/rims/ppermute | solution.py:364
  54.0 3.0 %collective-permute-start.3 = (bf16[8,192,128]{2,1,0:T(8,128)(2,1)}, bf16[8,192,128]{2,1,0:T(8,128)(2,1)S(1)}, u32[]{:S(2)}, u32[]{:S(2)}) collective-permute-start(bf16[8,192,128]{2,1,0:T(8,128)(2,1)} %get-tuple-element.30), channel_id=1, source_target_pairs={{1,2},{2,1},{5,6},{6,5},{9,10},{10,9},{13,14},{14,13},{17,18},{18,... | collective-permute-start | bytes 1179656 | tf_op jit(solution)/shard_map/rims/ppermute | solution.py:364
  72.1 9.5 %copy-start.4 = (bf16[8,208,128]{2,1,0:T(8,128)(2,1)}, bf16[8,208,128]{2,1,0:T(8,128)(2,1)S(1)}, u32[]{:S(2)}) copy-start(bf16[8,208,128]{2,1,0:T(8,128)(2,1)S(1)} %all_to_all.20.g_ref) | copy-start | bytes 1277956
  72.8 18.4 %all-to-all-start.3 = ((f32[4,1,128]{2,1,0:T(1,128)}), f32[4,1,128]{2,1,0:T(1,128)S(1)}, u32[]{:S(2)}, u32[]{:S(2)}) async-start(f32[4,1,128]{2,1,0:T(1,128)} %broadcast_in_dim.18), calls=%async_computation.3 | async-start | bytes 4096 | tf_op jit(solution)/shard_map/loss/all_to_all | solution.py:532
